TPU v7x, 256 devices: a whole 4x4x8 slice. The times are simulated.
256 devices in a mesh: row: 32 (over z, x), col: 8 (over y, core).
Axes of the slice: x: 4, y: 4, z: 8, core: 2. Of those that a mesh axis runs over, the one named last changes fastest.
Arguments:
- schur: float32 [2, 32768, 4096], P(None, 'row', 'col'), may hold values from -6 to 6
- lower: bfloat16 [2, 32768, 2048], P(None, 'row', 'col'), may hold values from -6 to 6
- upper: bfloat16 [2, 2048, 4096], P(None, 'row', 'col'), may hold values from -0.1875 to 0.1875
- tile_mask: int32 [2, 256, 16], P(None, 'row', 'col'), may hold values from 0 to 1, as said below
- row_map: int32 [2, 32768], P(None, 'row'), may hold values from 0 to 32767, as said below
- front: float32 [32768, 4096], P('row', 'col'), may hold values from -6 to 6
Outputs:
- front_out: float32 [32768, 4096], P('row', 'col')
Inputs may be any that keep to these rules, and one draw needn't show every extreme that they name: `tile_mask`: in every row of tiles of each child, each aligned pair of tile columns (2 j, 2 j + 1) holds exactly one 1. `row_map`: for each child a permutation of the 32768 rows. Of the 1024 rows of any aligned block, at least 16 and at most 48 map into any one aligned block of 1024 parent rows; some pair of blocks reaches 48.
All inputs are finite; a program needn't handle non-finite values.
Results may differ from a plain program's by a relative error of at most 0.0003.
Values may be sent and summed in bfloat16 or wider, within the bound.
A program may use at most 128 MiB of HBM per device.

v0:
```python
import jax
import jax.numpy as jnp
from jax import lax
from jax.sharding import Mesh
from jax.sharding import PartitionSpec as P

TILE = 128
ROW = ("row_0", "row_1")


def gathered_by_axis(array, axes, dim):
    result = array
    for number in range(len(axes) - 1, -1, -1):
        result = lax.all_gather(result, axes[number], axis=dim, tiled=True)
    return result


def build_send(contrib, maps, count):
    children, rows, width = contrib.shape
    cap = 3 * rows // (2 * count)
    target = maps // rows
    place = maps % rows
    onehot = (target[:, :, None] == jnp.arange(count, dtype=jnp.int32)[None, None, :]).astype(
        jnp.int32
    )
    ranks = jnp.cumsum(onehot, axis=1) - 1
    slot = jnp.sum(ranks * onehot, axis=2)
    flat = target * cap + slot
    child_ids = jnp.arange(children, dtype=jnp.int32)[:, None]
    values = jnp.zeros((children, count * cap, width), jnp.float32).at[child_ids, flat].set(contrib)
    places = (
        jnp.full((children, count * cap), float(rows), jnp.float32)
        .at[child_ids, flat]
        .set(place.astype(jnp.float32))
    )
    return (values.reshape(children, count, cap, width), places.reshape(children, count, cap))


def assemble(result, values, places):
    width = values.shape[-1]
    index = places.reshape(-1).astype(jnp.int32)
    return result.at[index].add(values.reshape(-1, width), mode="drop")


def shards(schur, lower, upper, tile_mask, row_map, front):
    children, rows, local_depth = lower.shape
    width = schur.shape[2]
    row_tiles = rows // TILE
    local_tiles = local_depth // TILE
    upper_full = gathered_by_axis(upper, ROW, 1)
    local_pairs = local_tiles // 2
    lower_six = lower.reshape(children, row_tiles, TILE, local_pairs, 2, TILE)
    weight_six = tile_mask.reshape(children, row_tiles, 1, local_pairs, 2, 1).astype(jnp.bfloat16)
    packed = jnp.sum(lower_six * weight_six, axis=4).reshape(children, rows, local_pairs * TILE)
    flags = tile_mask.reshape(children, row_tiles, local_pairs, 2)[..., 1].astype(jnp.bfloat16)
    packed_full, flags_full = (
        lax.all_gather(packed, "col", axis=2, tiled=True),
        lax.all_gather(flags, "col", axis=2, tiled=True),
    )
    total_pairs = flags_full.shape[2]
    upper_pairs = upper_full.reshape(children, total_pairs, 2, TILE, width)
    packed_five = packed_full.reshape(children, row_tiles, TILE, total_pairs, TILE)
    update = jnp.zeros((children, rows, width), jnp.float32)
    for parity in range(2):
        select = (flags_full == float(parity)).astype(jnp.bfloat16)
        chosen = (packed_five * select[:, :, None, :, None]).reshape(
            children, rows, total_pairs * TILE
        )
        panel = upper_pairs[:, :, parity].reshape(children, total_pairs * TILE, width)
        update = update + jnp.einsum(
            "cmk,ckw->cmw", chosen, panel, preferred_element_type=jnp.float32
        )
    contrib = schur - update
    count = lax.axis_size(ROW)
    result = front
    values, places = build_send(contrib, row_map, count)
    got_values, got_places = (
        lax.all_to_all(values, ROW, split_axis=1, concat_axis=1, tiled=True),
        lax.all_to_all(places, ROW, split_axis=1, concat_axis=1, tiled=True),
    )
    result = assemble(result, got_values, got_places)
    return result


def solution(mesh):
    split = Mesh(mesh.devices.reshape(8, 4, mesh.shape["col"]), ("row_0", "row_1", "col"))
    in_specs = (
        P(None, ROW, "col"),
        P(None, ROW, "col"),
        P(None, ROW, "col"),
        P(None, ROW, "col"),
        P(None, ROW),
        P(ROW, "col"),
    )
    out_specs = P(ROW, "col")
    return jax.shard_map(
        shards, mesh=split, in_specs=in_specs, out_specs=out_specs, check_vma=False
    )
```

profile of v0, /device:TPU:103, one launch (start us, length us, event | category | flops | bytes accessed | tf_op | source)
XLA Modules:
  0.0 343.6 jit_solution(4166249342058747314)
XLA Ops:
  6.6 3.2 copy.65
  9.8 10.8 %all_gather.14 = bf16[2,256,512]{2,1,0:T(8,128)(2,1)} all-gather(bf16[2,64,512]{2,1,0:T(8,128)(2,1)S(1)} %copy-done.4), channel_id=1, replica_groups=mesh['row_0'=8,'row_1'=4,'col'=8] {'row_1'}, dimensions={1}, use_global_device_ids=true | all-gather | bytes 655360 | tf_op jit(solution)/shard_map/all_gather | solution.py:14
  20.6 0.3 reshape.99
  20.9 0.1 copy.43
  21.0 3.7 %multiply_reduce_fusion = bf16[2,8,128,128]{3,2,1,0:T(8,128)(2,1)} fusion(bf16[2,8,128,1,2,128]{5,4,2,1,0,3:T(2,128)(2,1)S(1)} %reshape.99, bf16[2,8,2]{2,1,0:T(8,128)(2,1)S(1)} %copy.43), kind=kLoop, calls=%fused_computation.10 | loop fusion | flops 786432 | bytes 1572928 | tf_op jit(solution)/shard_map/reduce_sum | solution.py:54
  24.9 18.0 %reduce-window.6 = s32[2,32,8,128]{3,2,1,0:T(8,128)S(1)} reduce-window(s32[2,32,8,128]{3,2,1,0:T(8,128)S(1)} %fusion.9, s32[]{:T(128)} %constant.45.clone.1), window={size=1x1x1x128 pad=0_0x0_0x0_0x127_0}, to_apply=%region_0.0 | reduce-window | flops 8323072 | bytes 524292 | tf_op jit(solution)/shard_map/reduce-window
  42.9 0.1 slice.21
  43.0 0.2 copy.39
  43.3 0.1 add_add_fusion
  43.6 0.1 multiply_reduce_fusion.1
  43.7 0.1 and_reduce_fusion
  43.9 8.1 %scatter_custom_fusion.1 = f32[3072]{0:T(1024)S(1)} fusion(s32[2048]{0:T(1024)S(1)} %bitcast.58, f32[2048]{0:T(1024)S(1)} %bitcast.60, f32[]{:T(128)} %constant.43.clone.1), kind=kCustom, calls=%fused_computation.37 | custom fusion | bytes 12292
  52.0 0.6 copy.41
  52.6 9.4 %all-to-all-start = ((f32[2,32,48]{2,0,1:T(2,128)}), f32[2,32,48]{2,0,1:T(2,128)S(1)}, u32[]{:S(2)}, u32[]{:S(2)}) async-start(f32[2,32,48]{2,0,1:T(2,128)} %copy.41), calls=%async_computation | async-start | bytes 65536 | tf_op jit(solution)/shard_map/all_to_all | solution.py:79
  62.1 15.6 %all-gather = bf16[2,8,8,1]{1,0,3,2:T(2,128)(2,1)S(1)} all-gather(bf16[2,8,1,1]{1,0,3,2:T(2,128)(2,1)S(1)} %copy.44), channel_id=2, replica_groups=mesh['row_0'=8,'row_1'=4,'col'=8] {'col'}, dimensions={2}, use_global_device_ids=true | all-gather | bytes 288 | tf_op jit(solution)/shard_map/all_gather | solution.py:58
  77.7 0.1 copy.45
  77.8 2.6 mul.55
  80.3 7.3 %mul.56 = bf16[2,1024,1024]{2,1,0:T(8,128)(2,1)} reshape(bf16[2,8,128,8,128]{4,3,2,1,0:T(8,128)(2,1)} %mul.55) | data formatting | bytes 8388608 | tf_op jit(solution)/shard_map/mul | solution.py:66
  87.7 2.5 mul.52
  90.2 7.3 %mul.53 = bf16[2,1024,1024]{2,1,0:T(8,128)(2,1)} reshape(bf16[2,8,128,8,128]{4,3,2,1,0:T(8,128)(2,1)} %mul.52) | data formatting | bytes 8388608 | tf_op jit(solution)/shard_map/mul | solution.py:66
  97.5 4.0 %fusion.17 = (bf16[2,8,1,128,512]{4,3,2,1,0:T(8,128)(2,1)S(1)}, bf16[2,8,1,128,512]{4,3,2,1,0:T(8,128)(2,1)}) fusion(bf16[2,8,2,128,512]{4,3,2,1,0:T(8,128)(2,1)} %bitcast.50), kind=kLoop, calls=%fused_computation.43 | loop fusion | bytes 8388608 | tf_op jit(solution)/shard_map/slice | solution.py:69
  101.5 18.7 %all-gather.4.cloned.1.call-done = bf16[2,1024,1024]{2,1,0:T(8,128)(2,1)} async-done(((bf16[2,1024,128]{2,1,0:T(8,128)(2,1)}), bf16[2,1024,1024]{2,1,0:T(8,128)(2,1)}) %all-gather.4.cloned.1.call-update) | async-done | bytes 4194320 | tf_op jit(solution)/shard_map/all_gather | solution.py:57
  120.2 6.5 %fusion = f32[2,1024,512]{2,1,0:T(8,128)S(1)} fusion(bf16[2,1024,512]{2,1,0:T(8,128)(2,1)} %bitcast.53, bf16[2,1024,1024]{2,1,0:T(8,128)(2,1)} %all-gather.4.cloned.1.call-done, bf16[2,1024,1024]{2,1,0:T(8,128)(2,1)} %mul.56), kind=kOutput, calls=%fused_computation.4 | convolution fusion | flops 2149580800 | bytes 14680064 | tf_op jit(solution)/shard_map/cmk,ckw->cmw/dot_general | solution.py:70
  126.8 1.2 copy-done.2
  128.0 4.3 %add_subtract_fusion = f32[2,1024,512]{2,1,0:T(8,128)} fusion(f32[2,1024,512]{2,1,0:T(8,128)S(1)} %copy-done.1, f32[2,1024,512]{2,1,0:T(8,128)S(1)} %fusion, bf16[2,1024,512]{2,1,0:T(8,128)(2,1)S(1)} %bitcast.49, bf16[2,1024,1024]{2,1,0:T(8,128)(2,1)S(1)} %copy-done.2, bf16[2,1024,1024]{2,1,0:T(8,128)(2,1)S(1)} %copy-done), kind=kOutput, calls=%fused_computation.3 | convolution fusion | flops 2151677952 | bytes 23068672 | tf_op jit(solution)/shard_map/cmk,ckw->cmw/dot_general | solution.py:70
  132.2 12.7 %scatter_custom_fusion.2 = f32[3072,512]{1,0:T(8,128)} fusion(s32[2048]{0:T(1024)S(1)} %bitcast.59, f32[2048,512]{1,0:T(8,128)} %bitcast.51, f32[]{:T(128)} %constant.52.clone.1), kind=kCustom, calls=%fused_computation.8 | custom fusion | bytes 6291968
  144.9 6.7 %copy.49 = f32[2,32,48,512]{3,2,0,1:T(8,128)} copy(f32[2,32,48,512]{3,2,1,0:T(8,128)} %bitcast.47) | data formatting | bytes 12582912 | tf_op jit(solution)/shard_map/reshape | solution.py:36
  151.6 9.4 %all-to-all-start.1 = ((f32[2,32,48,512]{3,2,0,1:T(8,128)}), f32[2,32,48,512]{3,2,0,1:T(8,128)}, u32[]{:S(2)}, u32[]{:S(2)}) async-start(f32[2,32,48,512]{3,2,0,1:T(8,128)} %copy.49), calls=%async_computation.1 | async-start | bytes 12582912 | tf_op jit(solution)/shard_map/all_to_all | solution.py:78
  161.0 0.1 convert_element_type.48
  161.1 146.8 %all-to-all-done.1 = f32[2,32,48,512]{3,2,0,1:T(8,128)} async-done(((f32[2,32,48,512]{3,2,0,1:T(8,128)}), f32[2,32,48,512]{3,2,0,1:T(8,128)}, u32[]{:S(2)}, u32[]{:S(2)}) %all-to-all-start.1) | async-done | bytes 6291488 | tf_op jit(solution)/shard_map/all_to_all | solution.py:78
  308.0 6.8 %copy.50 = f32[2,32,48,512]{3,2,1,0:T(8,128)} copy(f32[2,32,48,512]{3,2,0,1:T(8,128)} %all-to-all-done.1) | data formatting | bytes 12582912 | tf_op jit(solution)/shard_map/all_to_all | solution.py:78
  314.7 22.1 %scatter_fusion = f32[1024,512]{1,0:T(8,128)} fusion(f32[1024,512]{1,0:T(8,128)} %copy.65, s32[3072]{0:T(1024)S(1)} %bitcast.55, f32[3072,512]{1,0:T(8,128)} %bitcast.48), kind=kCustom, calls=%fused_computation | custom fusion | flops 1572864 | bytes 18886656 | tf_op jit(solution)/shard_map/scatter-add | solution.py:42
  (44 shorter events, 0.6 us)
Async XLA Ops:
  6.5 3.2 copy-start.4
  6.5 14.1 %copy-start.3 = (bf16[2,1024,256]{2,1,0:T(8,128)(2,1)S(1)}, bf16[2,1024,256]{2,1,0:T(8,128)(2,1)}, u32[]{:S(2)}) copy-start(bf16[2,1024,256]{2,1,0:T(8,128)(2,1)} %param.7) | copy-start | bytes 3145732
  6.5 14.4 %copy-start.6 = (s32[2,8,2]{1,2,0:T(2,128)S(1)}, s32[2,8,2]{1,2,0:T(2,128)}, u32[]{:S(2)}) copy-start(s32[2,8,2]{1,2,0:T(2,128)} %param.9) | copy-start | bytes 388
  6.5 18.3 %copy-start.5 = (s32[2,1024]{1,0:T(2,128)S(1)}, s32[2,1024]{1,0:T(2,128)}, u32[]{:S(2)}) copy-start(s32[2,1024]{1,0:T(2,128)} %param.10) | copy-start | bytes 24580
  6.5 91.0 %all-gather.6.cloned.1.call-start = ((), (), s32[]{:S(2)}) async-start(), calls=%async_computation.3 | async-start | bytes 4718592 | tf_op jit(solution)/shard_map/all_gather | solution.py:14
  9.8 33.9 %copy-start.7 = (s32[2]{0:T(128)S(1)}, s32[2]{0:T(128)}, u32[]{:S(2)}) copy-start(s32[2]{0:T(128)} %constant.56) | copy-start | bytes 28
  9.8 34.0 %copy-start.8 = (s32[2]{0:T(128)S(1)}, s32[2]{0:T(128)}, u32[]{:S(2)}) copy-start(s32[2]{0:T(128)} %constant.59) | copy-start | bytes 28
  20.5 99.7 %all-gather.4.cloned.1.call-start = ((), (), s32[]{:S(2)}) async-start(), calls=%async_computation.2 | async-start | bytes 4718592 | tf_op jit(solution)/shard_map/all_gather | solution.py:57
  52.6 99.0 %all-to-all-start = ((f32[2,32,48]{2,0,1:T(2,128)}), f32[2,32,48]{2,0,1:T(2,128)S(1)}, u32[]{:S(2)}, u32[]{:S(2)}) async-start(f32[2,32,48]{2,0,1:T(2,128)} %copy.41), calls=%async_computation | async-start | bytes 65536 | tf_op jit(solution)/shard_map/all_to_all | solution.py:79
  120.2 6.5 %copy-start = (bf16[2,1024,1024]{2,1,0:T(8,128)(2,1)S(1)}, bf16[2,1024,1024]{2,1,0:T(8,128)(2,1)}, u32[]{:S(2)}) copy-start(bf16[2,1024,1024]{2,1,0:T(8,128)(2,1)} %mul.53) | copy-start | bytes 12582916
  120.2 6.5 %copy-start.1 = (f32[2,1024,512]{2,1,0:T(8,128)S(1)}, f32[2,1024,512]{2,1,0:T(8,128)}, u32[]{:S(2)}) copy-start(f32[2,1024,512]{2,1,0:T(8,128)} %param.6) | copy-start | bytes 12582916
  120.2 7.7 %copy-start.2 = (bf16[2,1024,1024]{2,1,0:T(8,128)(2,1)S(1)}, bf16[2,1024,1024]{2,1,0:T(8,128)(2,1)}, u32[]{:S(2)}) copy-start(bf16[2,1024,1024]{2,1,0:T(8,128)(2,1)} %all-gather.4.cloned.1.call-done) | copy-start | bytes 12582916
  151.6 156.3 %all-to-all-start.1 = ((f32[2,32,48,512]{3,2,0,1:T(8,128)}), f32[2,32,48,512]{3,2,0,1:T(8,128)}, u32[]{:S(2)}, u32[]{:S(2)}) async-start(f32[2,32,48,512]{3,2,0,1:T(8,128)} %copy.49), calls=%async_computation.1 | async-start | bytes 12582912 | tf_op jit(solution)/shard_map/all_to_all | solution.py:78
Sparse Core Ops, SparseCore 0:
  20.7 59.8 all-gather.5
  82.4 37.8 all-gather.3
where the time goes:
time: 344 us
  waiting for transfers between devices  166 us (48%)
  local copies, waits for them, and re-layouts  64 us (19%)
  other arithmetic  44.3 us (13%)
  blocking collectives  26.3 us (8%)
  starting transfers between devices  18.9 us (5%)
  between operations  13.7 us (4%)
  matrix products  10.8 us (3%)
    all_to_all x1, waiting for transfers between devices, shards(): lax.all_to_all(values, ROW, split_axis=1, concat_axis=1, tiled=True)  147 us
    unnamed x24, local copies, waits for them, and re-layouts  25.1 us
    scatter-add x1, other arithmetic, assemble(): return result.at[index].add(values.reshape(-1, width), mode='drop')  22.1 us
    mul x4, local copies, waits for them, and re-layouts, shards(): packed_five * select[:, :, None, :, None]  19.8 us
    all_gather x1, waiting for transfers between devices, shards(): lax.all_gather(packed, 'col', axis=2, tiled=True)  18.7 us
    another operation x2, other arithmetic  18.1 us
    all_gather x1, blocking collectives, shards(): lax.all_gather(flags, 'col', axis=2, tiled=True)  15.6 us
    dot_general x2, matrix products, shards(): jnp.einsum('cmk,ckw->cmw', chosen, panel, preferred_element_type=jnp.floa...  10.8 us
  transfers between devices with their start and end apart: 4, of which 2 were waited for; matrix products, arithmetic and copies ran while one was open for 25% of the time, Pallas kernels for 0%

commit v1 on v0

--- a/solution.py
+++ b/solution.py
@@ -6,6 +6,13 @@
 
 TILE = 128
 ROW = ("row_0", "row_1")
+
+
+def exchange_gather(x, axis, along):
+    peers = lax.axis_size(axis)
+    blocks = jnp.stack([x for _ in range(peers)])
+    blocks = lax.all_to_all(blocks, axis, split_axis=0, concat_axis=0)
+    return jnp.concatenate(blocks, axis=along)
 
 
 def gathered_by_axis(array, axes, dim):
@@ -54,7 +61,7 @@
     packed = jnp.sum(lower_six * weight_six, axis=4).reshape(children, rows, local_pairs * TILE)
     flags = tile_mask.reshape(children, row_tiles, local_pairs, 2)[..., 1].astype(jnp.bfloat16)
     packed_full, flags_full = (
-        lax.all_gather(packed, "col", axis=2, tiled=True),
+        exchange_gather(packed, "col", 2),
         lax.all_gather(flags, "col", axis=2, tiled=True),
     )
     total_pairs = flags_full.shape[2]

time: 344 us -> 363 us (1.055)
  waiting for transfers between devices: 166 us -> 146 us
  blocking collectives: 26.3 us -> 44 us
  starting transfers between devices: 18.9 us -> 27.5 us
  local copies, waits for them, and re-layouts: 64 us -> 72.6 us
  other arithmetic: 44.3 us -> 51.6 us
  matrix products: 10.8 us -> 6.68 us
    all_gather x1 -> x0, waiting for transfers between devices: 18.7 us -> none  [shards(): lax.all_gather(packed, 'col', axis=2, tiled=True)]
    all_gather x1, blocking collectives: 15.6 us -> 33.4 us  [shards(): lax.all_gather(flags, 'col', axis=2, tiled=True)]
    all_to_all x0 -> x1, starting transfers between devices: none -> 8.85 us  [exchange_gather(): blocks = lax.all_to_all(blocks, axis, split_axis=0, concat_axis=0)]
    mul x0 -> x1, other arithmetic: none -> 8.03 us  [shards(): packed_five * select[:, :, None, :, None]]
    all_to_all x0 -> x1, local copies, waits for them, and re-layouts: none -> 6.26 us  [exchange_gather(): blocks = lax.all_to_all(blocks, axis, split_axis=0, concat_axis=0)]
    dot_general x2, matrix products: 10.8 us -> 6.68 us  [shards(): jnp.einsum('cmk,ckw->cmw', chosen, panel, preferred_element_type=jnp.floa...]
  transfers between devices with their start and end apart: 4 -> 4, of which waited for: 2 -> 1; matrix products, arithmetic and copies ran while one was open for 25% -> 27% of each run, Pallas kernels for 0% -> 0%
where the time goes in v1:
time: 363 us; the launch traced here: 362 us
  waiting for transfers between devices  146 us (40%)
  local copies, waits for them, and re-layouts  72.6 us (20%)
  other arithmetic  51.6 us (14%)
  blocking collectives  44 us (12%)
  starting transfers between devices  27.5 us (8%)
  between operations  13.6 us (4%)
  matrix products  6.68 us (2%)
    all_to_all x1, waiting for transfers between devices, shards(): lax.all_to_all(values, ROW, split_axis=1, concat_axis=1, tiled=True)  145 us
    all_gather x1, blocking collectives, shards(): lax.all_gather(flags, 'col', axis=2, tiled=True)  33.4 us
    unnamed x24, local copies, waits for them, and re-layouts  25.8 us
    scatter-add x1, other arithmetic, assemble(): return result.at[index].add(values.reshape(-1, width), mode='drop')  22.1 us
    mul x4, local copies, waits for them, and re-layouts, shards(): packed_five * select[:, :, None, :, None]  19.7 us
    another operation x2, other arithmetic  18.1 us
    all_gather x1, blocking collectives, gathered_by_axis(): result = lax.all_gather(result, axes[number], axis=dim, tiled=True)  10.6 us
    all_to_all x1, starting transfers between devices, shards(): lax.all_to_all(places, ROW, split_axis=1, concat_axis=1, tiled=True)  9.38 us
  transfers between devices with their start and end apart: 4, of which 1 were waited for; matrix products, arithmetic and copies ran while one was open for 27% of the time, Pallas kernels for 0%

profile of v1, /device:TPU:103, one launch (start us, length us, event | category | flops | bytes accessed | tf_op | source)
XLA Modules:
  0.0 361.5 jit_solution(12113729253234978242)
XLA Ops:
  6.5 3.2 copy.77
  9.7 10.6 %all_gather.10 = bf16[2,256,512]{2,1,0:T(8,128)(2,1)} all-gather(bf16[2,64,512]{2,1,0:T(8,128)(2,1)S(1)} %copy-done.4), channel_id=1, replica_groups=mesh['row_0'=8,'row_1'=4,'col'=8] {'row_1'}, dimensions={1}, use_global_device_ids=true | all-gather | bytes 655360 | tf_op jit(solution)/shard_map/all_gather | solution.py:21
  20.4 0.3 reshape.102
  20.7 0.1 copy.48
  20.8 2.9 multiply_reduce_fusion
  23.8 2.8 stack.3
  26.5 8.9 %all-to-all-start.1 = ((bf16[8,2,1024,128]{3,2,1,0:T(8,128)(2,1)}), bf16[8,2,1024,128]{3,2,1,0:T(8,128)(2,1)}, u32[]{:S(2)}, u32[]{:S(2)}) async-start(bf16[8,2,1024,128]{3,2,1,0:T(8,128)(2,1)} %stack.3), calls=%async_computation.1 | async-start | bytes 8388608 | tf_op jit(solution)/shard_map/all_to_all | solution.py:14
  35.5 18.0 %reduce-window.6 = s32[2,32,8,128]{3,2,1,0:T(8,128)S(1)} reduce-window(s32[2,32,8,128]{3,2,1,0:T(8,128)S(1)} %fusion.3, s32[]{:T(128)} %constant.45.clone.1), window={size=1x1x1x128 pad=0_0x0_0x0_0x127_0}, to_apply=%region_0.0 | reduce-window | flops 8323072 | bytes 524292 | tf_op jit(solution)/shard_map/reduce-window
  53.5 0.1 slice.21
  53.6 0.2 copy.44
  53.9 0.1 add_add_fusion
  54.5 33.4 %all-gather = bf16[2,8,8,1]{1,0,3,2:T(2,128)(2,1)S(1)} all-gather(bf16[2,8,1,1]{1,0,3,2:T(2,128)(2,1)S(1)} %copy.50), channel_id=2, replica_groups=mesh['row_0'=8,'row_1'=4,'col'=8] {'col'}, dimensions={2}, use_global_device_ids=true | all-gather | bytes 288 | tf_op jit(solution)/shard_map/all_gather | solution.py:65
  88.0 2.5 mul.52
  90.5 7.3 %mul.53 = bf16[2,1024,1024]{1,2,0:T(8,128)(2,1)} reshape(bf16[2,8,128,8,128]{2,1,4,3,0:T(8,128)(2,1)} %mul.52) | data formatting | bytes 8388608 | tf_op jit(solution)/shard_map/mul | solution.py:73
  97.9 2.6 mul.55
  100.5 7.3 %mul.56 = bf16[2,1024,1024]{1,2,0:T(8,128)(2,1)} reshape(bf16[2,8,128,8,128]{2,1,4,3,0:T(8,128)(2,1)} %mul.55) | data formatting | bytes 8388608 | tf_op jit(solution)/shard_map/mul | solution.py:73
  107.8 8.1 %scatter_custom_fusion.1 = f32[3072]{0:T(1024)S(1)} fusion(s32[2048]{0:T(1024)S(1)} %bitcast.69, f32[2048]{0:T(1024)S(1)} %bitcast.71, f32[]{:T(128)} %constant.43.clone.1), kind=kCustom, calls=%fused_computation.35 | custom fusion | bytes 12292
  116.0 0.6 copy.46
  116.6 9.4 %all-to-all-start = ((f32[2,32,48]{2,0,1:T(2,128)}), f32[2,32,48]{2,0,1:T(2,128)S(1)}, u32[]{:S(2)}, u32[]{:S(2)}) async-start(f32[2,32,48]{2,0,1:T(2,128)} %copy.46), calls=%async_computation | async-start | bytes 65536 | tf_op jit(solution)/shard_map/all_to_all | solution.py:86
  126.0 6.3 %copy.49 = bf16[8,2,1024,128]{2,3,0,1:T(8,128)(2,1)} copy(bf16[8,2,1024,128]{3,2,1,0:T(8,128)(2,1)} %all-to-all-done.1) | data formatting | bytes 8388608 | tf_op jit(solution)/shard_map/all_to_all | solution.py:14
  132.3 8.0 %bitcast_multiply_fusion = (bf16[2,1024,1024]{1,2,0:T(8,128)(2,1)}, bf16[2,1024,1024]{1,2,0:T(8,128)(2,1)}) fusion(bf16[2,1024,1024]{1,2,0:T(8,128)(2,1)} %mul.56, bf16[8,2,1024,128]{2,3,0,1:T(8,128)(2,1)} %copy.49, bf16[2,1024,1024]{1,2,0:T(8,128)(2,1)} %mul.53), kind=kLoop, calls=%fused_computation.3 | loop fusion | flops 4194304 | bytes 20971520 | tf_op jit(solution)/shard_map/mul | solution.py:73
  140.3 2.7 fusion.11
  143.0 0.8 copy-done.1
  143.7 2.4 fusion.12
  146.1 1.1 copy-done.2
  147.2 4.3 %add_subtract_fusion = f32[2,1024,512]{2,1,0:T(8,128)} fusion(f32[2,1024,512]{2,1,0:T(8,128)S(1)} %copy-done.2, f32[2,1024,512]{2,1,0:T(8,128)S(1)} %fusion.12, bf16[2,1024,1024]{1,2,0:T(8,128)(2,1)S(1)} %copy-done, bf16[2,1024,512]{2,1,0:T(8,128)(2,1)S(1)} %bitcast.60), kind=kOutput, calls=%fused_computation.5 | convolution fusion | flops 2149580800 | bytes 18874368 | tf_op jit(solution)/shard_map/cmk,ckw->cmw/dot_general | solution.py:77
  151.5 12.7 %scatter_custom_fusion.2 = f32[3072,512]{1,0:T(8,128)} fusion(s32[2048]{0:T(1024)S(1)} %bitcast.70, f32[2048,512]{1,0:T(8,128)} %bitcast.62, f32[]{:T(128)} %constant.52.clone.1), kind=kCustom, calls=%fused_computation.6 | custom fusion | bytes 6291968
  164.2 6.7 %copy.59 = f32[2,32,48,512]{3,2,0,1:T(8,128)} copy(f32[2,32,48,512]{3,2,1,0:T(8,128)} %bitcast.58) | data formatting | bytes 12582912 | tf_op jit(solution)/shard_map/reshape | solution.py:43
  170.9 9.3 %all-to-all-start.2 = ((f32[2,32,48,512]{3,2,0,1:T(8,128)}), f32[2,32,48,512]{3,2,0,1:T(8,128)}, u32[]{:S(2)}, u32[]{:S(2)}) async-start(f32[2,32,48,512]{3,2,0,1:T(8,128)} %copy.59), calls=%async_computation.2 | async-start | bytes 12582912 | tf_op jit(solution)/shard_map/all_to_all | solution.py:85
  180.4 145.5 %all-to-all-done.2 = f32[2,32,48,512]{3,2,0,1:T(8,128)} async-done(((f32[2,32,48,512]{3,2,0,1:T(8,128)}), f32[2,32,48,512]{3,2,0,1:T(8,128)}, u32[]{:S(2)}, u32[]{:S(2)}) %all-to-all-start.2) | async-done | bytes 6291488 | tf_op jit(solution)/shard_map/all_to_all | solution.py:85
  325.8 6.8 %copy.60 = f32[2,32,48,512]{3,2,1,0:T(8,128)} copy(f32[2,32,48,512]{3,2,0,1:T(8,128)} %all-to-all-done.2) | data formatting | bytes 12582912 | tf_op jit(solution)/shard_map/all_to_all | solution.py:85
  332.6 22.1 %scatter_fusion = f32[1024,512]{1,0:T(8,128)} fusion(f32[1024,512]{1,0:T(8,128)} %copy.77, s32[3072]{0:T(1024)S(1)} %bitcast.66, f32[3072,512]{1,0:T(8,128)} %bitcast.59), kind=kCustom, calls=%fused_computation | custom fusion | flops 1572864 | bytes 18886656 | tf_op jit(solution)/shard_map/scatter-add | solution.py:49
  (48 shorter events, 1.0 us)
Async XLA Ops:
  6.5 3.2 copy-start.4
  6.5 13.8 %copy-start.3 = (bf16[2,1024,256]{2,1,0:T(8,128)(2,1)S(1)}, bf16[2,1024,256]{2,1,0:T(8,128)(2,1)}, u32[]{:S(2)}) copy-start(bf16[2,1024,256]{2,1,0:T(8,128)(2,1)} %param.7) | copy-start | bytes 3145732
  6.5 14.1 %copy-start.6 = (s32[2,8,2]{1,2,0:T(2,128)S(1)}, s32[2,8,2]{1,2,0:T(2,128)}, u32[]{:S(2)}) copy-start(s32[2,8,2]{1,2,0:T(2,128)} %param.9) | copy-start | bytes 388
  6.5 133.8 %all-gather.3.cloned.1.call-start = ((), (), s32[]{:S(2)}) async-start(), calls=%async_computation.3 | async-start | bytes 4718592 | tf_op jit(solution)/shard_map/all_gather | solution.py:21
  26.5 8.9 %copy-start.5 = (s32[2,1024]{1,0:T(2,128)S(1)}, s32[2,1024]{1,0:T(2,128)}, u32[]{:S(2)}) copy-start(s32[2,1024]{1,0:T(2,128)} %param.10) | copy-start | bytes 24580
  26.5 27.7 %copy-start.7 = (s32[2]{0:T(128)S(1)}, s32[2]{0:T(128)}, u32[]{:S(2)}) copy-start(s32[2]{0:T(128)} %constant.56) | copy-start | bytes 28
  26.5 27.8 %copy-start.8 = (s32[2]{0:T(128)S(1)}, s32[2]{0:T(128)}, u32[]{:S(2)}) copy-start(s32[2]{0:T(128)} %constant.59) | copy-start | bytes 28
  26.5 90.1 %all-to-all-start.1 = ((bf16[8,2,1024,128]{3,2,1,0:T(8,128)(2,1)}), bf16[8,2,1024,128]{3,2,1,0:T(8,128)(2,1)}, u32[]{:S(2)}, u32[]{:S(2)}) async-start(bf16[8,2,1024,128]{3,2,1,0:T(8,128)(2,1)} %stack.3), calls=%async_computation.1 | async-start | bytes 8388608 | tf_op jit(solution)/shard_map/all_to_all | solution.py:14
  116.6 54.3 %all-to-all-start = ((f32[2,32,48]{2,0,1:T(2,128)}), f32[2,32,48]{2,0,1:T(2,128)S(1)}, u32[]{:S(2)}, u32[]{:S(2)}) async-start(f32[2,32,48]{2,0,1:T(2,128)} %copy.46), calls=%async_computation | async-start | bytes 65536 | tf_op jit(solution)/shard_map/all_to_all | solution.py:86
  140.3 3.5 copy-start.1
  143.7 2.4 copy-start
  143.7 3.5 copy-start.2
  170.9 154.9 %all-to-all-start.2 = ((f32[2,32,48,512]{3,2,0,1:T(8,128)}), f32[2,32,48,512]{3,2,0,1:T(8,128)}, u32[]{:S(2)}, u32[]{:S(2)}) async-start(f32[2,32,48,512]{3,2,0,1:T(8,128)} %copy.59), calls=%async_computation.2 | async-start | bytes 12582912 | tf_op jit(solution)/shard_map/all_to_all | solution.py:85
Sparse Core Ops, SparseCore 0:
  20.5 59.1 all-gather.2
